TPU v7x, 32 devices: a whole 2x2x4 slice. The times are simulated.
32 devices in a mesh: dp: 8 (over y, x, core), seq: 4 (over z).
Axes of the slice: x: 2, y: 2, z: 4, core: 2. Of those that a mesh axis runs over, the one named last changes fastest.
Arguments:
- tokens: bfloat16 [8, 2048, 768], P('dp', 'seq'), may hold values from -6 to 6
- cotangent: bfloat16 [8, 2048, 768], P('dp', 'seq'), may hold values from -6 to 6
- segment_ids: int32 [8, 2048], P('dp', 'seq'), may hold values from 0 to 7, as said below
- doc_starts: int32 [8, 2048], P('dp', 'seq'), may hold values from 0 to 1, as said below
- valid_mask: int32 [8, 2048], P('dp', 'seq'), may hold values from 0 to 1
- step_number: int32 [1], replicated, may hold values from 1 to 64
- learn_rate: float32 [1], replicated, may hold values from 0.001 to 0.004
- norm_gain: float32 [768], replicated, may hold values from 0.5 to 1.5
- in_weight: bfloat16 [768, 3352], replicated, may hold values from -0.21875 to 0.21875
- conv_weight: float32 [4, 1792], replicated, may hold values from -3 to 3
- conv_bias: float32 [1792], replicated, may hold values from -1.75 to 1.75
- dt_bias: float32 [24], replicated, may hold values from -6 to -2
- a_log: float32 [24], replicated, may hold values from -1 to 2.5
- skip_d: float32 [24], replicated, may hold values from 0.5 to 1.5
- gate_gain: float32 [1536], replicated, may hold values from 0.5 to 1.5
- out_weight: bfloat16 [1536, 768], replicated, may hold values from -0.15625 to 0.15625
- in_momentum: float32 [768, 3352], P('seq'), may hold values from -6 to 6
- out_momentum: float32 [1536, 768], P(None, 'seq'), may hold values from -448 to 448
Outputs:
- output: bfloat16 [8, 2048, 768], P('dp', 'seq')
- input_grad: bfloat16 [8, 2048, 768], P('dp', 'seq')
- new_in_weight: bfloat16 [768, 3352], replicated
- new_out_weight: bfloat16 [1536, 768], replicated
- new_in_momentum: float32 [768, 3352], P('seq')
- new_out_momentum: float32 [1536, 768], P(None, 'seq')
- norm_gain_grad: float32 [768], replicated
- conv_weight_grad: float32 [4, 1792], replicated
- conv_bias_grad: float32 [1792], replicated
- dt_bias_grad: float32 [24], replicated
- a_log_grad: float32 [24], replicated
- skip_grad: float32 [24], replicated
- gate_gain_grad: float32 [1536], replicated
- output_rms: float32 [1], replicated
- mixer_rms: float32 [1], replicated
Inputs may be any that keep to these rules, and one draw needn't show every extreme that they name: Within each sequence segment_ids never fall, are 0 at the first position and rise by one exactly where doc_starts is 1; every sequence holds exactly 8 documents. `doc_starts`: 1 at the first position of every sequence; exactly 8 ones in every sequence.
All inputs are finite; a program needn't handle non-finite values.
Results may differ from a plain program's by a relative error of at most 0.0066.
The roundings to bfloat16 on the way count: a program that leaves them out, or rounds other values in their place, can miss the bound.
Values may be sent and summed in bfloat16 or wider, within the bound.
A program may use at most 192 MiB of HBM per device.

v0:
```python
import jax
import jax.numpy as jnp
from jax import lax
from jax.sharding import PartitionSpec as P

epsilon = 1e-05
highest = lax.Precision.HIGHEST


def shifted(block, axis, distance):
    devices = range(lax.axis_size(axis))
    route = [(i - distance, i) for i in devices if i - distance in devices]
    return lax.ppermute(block, axis, route)


def entering(value, axis, join, neutral):
    place = lax.axis_index(axis)
    gathered = jax.tree.map(
        lambda a, kind: lax.all_gather(a.astype(kind), axis), value, (jnp.bfloat16, jnp.bfloat16)
    )
    state = jax.tree.map(lambda a, e: jnp.zeros_like(a) + jnp.asarray(e, a.dtype), value, neutral)

    def one(step, state):
        return join(
            state,
            jax.tree.map(
                lambda a, own: lax.dynamic_index_in_dim(a, step, 0, False).astype(own.dtype),
                gathered,
                value,
            ),
        )

    return lax.fori_loop(0, place, one, state)


def carried_in(value, axis, combine, identity):
    length, mine = (lax.axis_size(axis), lax.axis_index(axis))
    everything = jax.tree.map(lambda part: lax.all_gather(part, axis), value)
    start = jax.tree.map(
        lambda part, zero: jnp.broadcast_to(jnp.asarray(zero, part.dtype), part.shape),
        value,
        identity,
    )

    def step(k, before):
        at = length - 1 - k
        reached = at > mine
        new = combine(before, jax.tree.map(lambda part: part[at], everything))
        return jax.tree.map(lambda a, b: jnp.where(reached, a, b), new, before)

    return lax.fori_loop(0, length, step, start)


def pre_norm(values, gain_values):
    return (
        values
        * lax.rsqrt(jnp.mean(values * values, axis=-1, keepdims=True) + epsilon)
        * gain_values
    )


def compose(earlier, later):
    return (earlier[0] * later[0], later[0][:, :, None, None] * earlier[1] + later[1])


def local(
    tokens,
    cotangent,
    segment_ids,
    doc_starts,
    valid_mask,
    step_number,
    learn_rate,
    norm_gain,
    in_weight,
    conv_weight,
    conv_bias,
    dt_bias,
    a_log,
    skip_d,
    gate_gain,
    out_weight,
    in_momentum,
    out_momentum,
):
    seq_count, piece_size, model_width = tokens.shape
    head_count = dt_bias.shape[0]
    tap_count, channels = conv_weight.shape
    inner_width = gate_gain.shape[0]
    state_width = (channels - inner_width) // 2
    head_width = inner_width // head_count
    proj_width = in_weight.shape[1]
    row_count = seq_count * piece_size
    inputs = tokens.astype(jnp.float32)
    normed_in, back_pre = jax.vjp(pre_norm, inputs, norm_gain)
    normed_low = normed_in.astype(jnp.bfloat16).reshape(row_count, model_width)
    projected = jnp.dot(normed_low, in_weight, preferred_element_type=jnp.float32).reshape(
        seq_count, piece_size, proj_width
    )
    gate_in = projected[:, :, :inner_width]
    conv_in = projected[:, :, inner_width : inner_width + channels]
    dt_raw = projected[:, :, inner_width + channels :]
    seg_float = segment_ids.astype(jnp.float32)
    prev_rows, prev_seg = shifted(
        (conv_in[:, piece_size - tap_count + 1 :], seg_float[:, piece_size - tap_count + 1 :]),
        "seq",
        1,
    )
    padded = jnp.concatenate([prev_rows, conv_in], axis=1)
    seg_pad = jnp.concatenate([prev_seg, seg_float], axis=1)
    masks = [
        (seg_pad[:, k : k + piece_size] == seg_float).astype(jnp.float32)[:, :, None]
        for k in range(tap_count)
    ]

    def conv_part(padded_in, taps_in, bias_in, raw_in, dt_bias_in, a_log_in):
        summed = bias_in + jnp.zeros((seq_count, piece_size, channels), jnp.float32)
        for k in range(tap_count):
            summed = summed + padded_in[:, k : k + piece_size] * masks[k] * taps_in[k]
        activated = jax.nn.silu(summed)
        signal = activated[:, :, :inner_width].reshape(
            seq_count, piece_size, head_count, head_width
        )
        writer = activated[:, :, inner_width : inner_width + state_width]
        reader = activated[:, :, inner_width + state_width :]
        step_size = jax.nn.softplus(raw_in + dt_bias_in)
        return (signal, writer, reader, step_size, -jnp.exp(a_log_in) * step_size)

    (signal, writer, reader, step_size, log_decay), back_conv = jax.vjp(
        conv_part, padded, conv_weight, conv_bias, dt_raw, dt_bias, a_log
    )
    counter = jnp.cumsum(doc_starts, axis=1)
    positions = jnp.arange(piece_size)
    causal = positions[:, None] >= positions[None, :]
    same_doc = (counter[:, :, None] == counter[:, None, :]) & causal[None]
    first_doc = (counter == 0)[:, :, None]
    last_doc = (counter == counter[:, -1:])[:, :, None]
    untouched = (counter[:, -1] == 0)[:, None]

    def end_state(signal_in, writer_in, step_in, decay_in):
        cumulative = jnp.cumsum(decay_in, axis=1)
        final_log = cumulative[:, -1]
        keeping = jnp.where(untouched, jnp.exp(final_log), 0.0)
        tails = jnp.where(last_doc, jnp.exp(final_log[:, None] - cumulative), 0.0) * step_in
        fresh_state = jnp.einsum(
            "slh,slhp,sln->shpn", tails, signal_in, writer_in, precision=highest
        )
        return (keeping, fresh_state)

    def piece_out(signal_in, writer_in, reader_in, step_in, decay_in, incoming_in):
        cumulative = jnp.cumsum(decay_in, axis=1)
        by_head = jnp.transpose(cumulative, (0, 2, 1))
        gaps = by_head[:, :, :, None] - by_head[:, :, None, :]
        decays = jnp.exp(jnp.where(same_doc[:, None], gaps, -1e30))
        scores = jnp.einsum("stn,sun->stu", reader_in, writer_in, precision=highest)
        weighted = scores[:, None] * decays
        inner_part = jnp.einsum(
            "shtu,suhp->sthp", weighted, signal_in * step_in[..., None], precision=highest
        )
        entries = jnp.where(first_doc, jnp.exp(cumulative), 0.0)
        carried = (
            jnp.einsum("stn,shpn->sthp", reader_in, incoming_in, precision=highest)
            * entries[..., None]
        )
        return inner_part + carried

    (keeping, fresh_state), back_end = jax.vjp(end_state, signal, writer, step_size, log_decay)
    identity = (jnp.ones_like(keeping), jnp.zeros_like(fresh_state))
    _, incoming = entering((keeping, fresh_state), "seq", compose, identity)
    ssm_out, back_out = jax.vjp(piece_out, signal, writer, reader, step_size, log_decay, incoming)

    def gate_norm(ssm_in, signal_in, skip_in, gate_values, gain_values):
        mixer_in = (ssm_in + skip_in[:, None] * signal_in).reshape(
            seq_count, piece_size, inner_width
        )
        gated_out = mixer_in * jax.nn.silu(gate_values)
        return (
            gated_out
            * lax.rsqrt(jnp.mean(gated_out * gated_out, axis=-1, keepdims=True) + epsilon)
            * gain_values
        )

    gate_normed, back_gate = jax.vjp(gate_norm, ssm_out, signal, skip_d, gate_in, gate_gain)
    gate_low = gate_normed.astype(jnp.bfloat16).reshape(row_count, inner_width)
    mixed = jnp.dot(gate_low, out_weight, preferred_element_type=jnp.float32).reshape(
        seq_count, piece_size, model_width
    )
    block_out = inputs + mixed
    valid_float = valid_mask.astype(jnp.float32)
    out_square = jnp.sum(valid_float * jnp.sum(block_out * block_out, axis=-1))
    mix_square = jnp.sum(valid_float * jnp.sum(mixed * mixed, axis=-1))
    valid_count = jnp.sum(valid_float)
    out_grad = cotangent.astype(jnp.float32) * valid_float[:, :, None]
    out_low = out_grad.astype(jnp.bfloat16).reshape(row_count, model_width)
    gate_grad = lax.dot_general(
        out_low, out_weight, (((1,), (1,)), ((), ())), preferred_element_type=jnp.float32
    ).reshape(seq_count, piece_size, inner_width)
    ssm_grad, signal_grad_gate, skip_grad, gate_in_grad, gate_gain_grad = back_gate(gate_grad)
    signal_grad_out, writer_grad_out, reader_grad, step_grad_out, decay_grad_out, state_grad = (
        back_out(ssm_grad)
    )
    _, later_grad = carried_in((keeping, state_grad), "seq", compose, identity)
    keeping_grad = jnp.sum(later_grad * incoming, axis=(2, 3))
    signal_grad_end, writer_grad_end, step_grad_end, decay_grad_end = back_end(
        (keeping_grad, later_grad)
    )
    padded_grad, conv_weight_grad, conv_bias_grad, dt_raw_grad, dt_bias_grad, a_log_grad = (
        back_conv(
            (
                signal_grad_gate + signal_grad_out + signal_grad_end,
                writer_grad_out + writer_grad_end,
                reader_grad,
                step_grad_out + step_grad_end,
                decay_grad_out + decay_grad_end,
            )
        )
    )
    rim_grad = shifted(padded_grad[:, : tap_count - 1].astype(jnp.bfloat16), "seq", -1).astype(
        jnp.float32
    )
    conv_in_grad = padded_grad[:, tap_count - 1 :] + jnp.pad(
        rim_grad, ((0, 0), (piece_size - tap_count + 1, 0), (0, 0))
    )
    proj_grad = (
        jnp.concatenate([gate_in_grad, conv_in_grad, dt_raw_grad], axis=2)
        .astype(jnp.bfloat16)
        .reshape(row_count, proj_width)
    )
    normed_grad = lax.dot_general(
        proj_grad, in_weight, (((1,), (1,)), ((), ())), preferred_element_type=jnp.float32
    ).reshape(seq_count, piece_size, model_width)
    input_grad_pre, norm_gain_grad = back_pre(normed_grad)
    input_grad = (out_grad + input_grad_pre).astype(jnp.bfloat16)
    share_rows = model_width // lax.axis_size("seq")
    in_part = lax.dot_general(
        normed_low, proj_grad, (((0,), (0,)), ((), ())), preferred_element_type=jnp.float32
    )
    out_part = lax.dot_general(
        out_low, gate_low, (((0,), (0,)), ((), ())), preferred_element_type=jnp.float32
    )
    whole_grad = lax.psum(jnp.concatenate([in_part, out_part], axis=1), "dp")
    grad_share = lax.psum_scatter(whole_grad, "seq", scatter_dimension=0, tiled=True)
    step_float = step_number[0].astype(jnp.float32)
    rate_now = learn_rate[0] * step_float / (step_float + 16.0)
    new_in_momentum = 0.5 * in_momentum + grad_share[:, :proj_width]
    new_out_momentum = 0.5 * out_momentum + jnp.transpose(grad_share[:, proj_width:])
    first_row = lax.axis_index("seq") * share_rows
    own_in = lax.dynamic_slice_in_dim(in_weight, first_row, share_rows, 0).astype(jnp.float32)
    own_out = lax.dynamic_slice_in_dim(out_weight, first_row, share_rows, 1).astype(jnp.float32)
    new_in_part = (own_in - rate_now * new_in_momentum).astype(jnp.bfloat16)
    new_out_part = (own_out - rate_now * new_out_momentum).astype(jnp.bfloat16)
    new_in_weight, new_out_weight = (
        lax.all_gather(new_in_part, "seq", axis=0, tiled=True),
        lax.all_gather(new_out_part, "seq", axis=1, tiled=True),
    )
    (
        norm_gain_total,
        conv_weight_total,
        conv_bias_total,
        dt_bias_total,
        a_log_total,
        skip_total,
        gate_gain_total,
        out_square_total,
        mix_square_total,
        valid_total,
    ) = lax.psum(
        (
            norm_gain_grad,
            conv_weight_grad,
            conv_bias_grad,
            dt_bias_grad,
            a_log_grad,
            skip_grad,
            gate_gain_grad,
            out_square,
            mix_square,
            valid_count,
        ),
        ("dp", "seq"),
    )
    denominator = jnp.maximum(valid_total, 1.0) * model_width
    output_rms = jnp.sqrt(out_square_total / denominator).reshape(1)
    mixer_rms = jnp.sqrt(mix_square_total / denominator).reshape(1)
    return (
        block_out.astype(jnp.bfloat16),
        input_grad,
        new_in_weight,
        new_out_weight,
        new_in_momentum,
        new_out_momentum,
        norm_gain_total,
        conv_weight_total,
        conv_bias_total,
        dt_bias_total,
        a_log_total,
        skip_total,
        gate_gain_total,
        output_rms,
        mixer_rms,
    )


def solution(mesh):
    placed = (
        P("dp", "seq", None),
        P("dp", "seq", None),
        P("dp", "seq"),
        P("dp", "seq"),
        P("dp", "seq"),
        P(),
        P(),
        P(),
        P(),
        P(),
        P(),
        P(),
        P(),
        P(),
        P(),
        P(),
        P("seq", None),
        P(None, "seq"),
    )
    return jax.shard_map(
        local,
        mesh=mesh,
        in_specs=placed,
        out_specs=(
            P("dp", "seq", None),
            P("dp", "seq", None),
            P(),
            P(),
            P("seq", None),
            P(None, "seq"),
            P(),
            P(),
            P(),
            P(),
            P(),
            P(),
            P(),
            P(),
            P(),
        ),
        check_vma=False,
    )
```

profile of v0, /device:TPU:0, one launch (start us, length us, event | category | flops | bytes accessed | tf_op | source)
XLA Modules:
  0.0 885.2 jit_solution(818629642145929513)
XLA Ops:
  9.2 5.5 convolution_bitcast_fusion
  14.8 4.9 collective-permute-start
  19.9 3.5 collective-permute-start.1
  25.9 4.2 slice.132
  36.3 11.6 %fusion.26 = (f32[1,512,1792]{2,1,0:T(8,128)S(1)}, f32[1,512,1792]{2,1,0:T(8,128)}) fusion(f32[1792]{0:T(1024)S(1)} %get-tuple-element.401, f32[1,512,1792]{2,1,0:T(8,128)} %slice.132, f32[512]{0:T(512)S(1)} %bitcast.377, f32[1792]{0:T(1024)S(1)} %get-tuple-element.402, f32[512]{0:T(512)S(1)} %bitcast.374, f32[1,3,1792]{2,1,0:T(4,128)S(1)} %copy.241, ...), kind=kLoop, calls=%fused_computation.50 | loop fusion | flops 17432576 | bytes 11075584 | tf_op jit(solution)/shard_map/jvp(jit(silu))/mul | solution.py:120
  54.3 4.3 fusion.70
  68.0 3.5 copy.254
  71.5 9.9 %all_gather.26 = bf16[4,1,24]{2,1,0:T(2,128)(2,1)} all-gather(bf16[1,1,24]{2,1,0:T(2,128)(2,1)} %get-tuple-element.453), channel_id=1, replica_groups=mesh['dp'=8,'seq'=4] {'seq'}, dimensions={0}, use_global_device_ids=true | all-gather | bytes 240 | tf_op jit(solution)/shard_map/all_gather | solution.py:19
  87.5 7.6 all-gather.11.cloned.1.call-done
  96.4 4.0 fusion.88
  100.5 29.3 %fusion.30 = f32[1,512,24,64]{1,3,2,0:T(8,128)} fusion(f32[1,512,24,64]{1,3,2,0:T(8,128)S(1)} %bitcast.337, f32[512,24,64]{0,2,1:T(8,128)S(1)} %fusion.88, f32[24]{0:T(128)S(1)} %copy-done.89, f32[512,24]{0,1:T(8,128)S(1)} %copy-done.35, f32[24,512]{1,0:T(8,128)S(1)} %copy-done.45, f32[512,512]{1,0:T(8,128)S(1)} %copy-done.27, ...), kind=kOutput, calls=%fused_computation.59 | convolution fusion | flops 4854644736 | bytes 14041184 | tf_op jit(solution)/shard_map/jvp(shtu,suhp->sthp)/dot_general | solution.py:157
  129.8 3.6 copy.252
  133.4 4.0 multiply_reduce_fusion.7
  141.5 5.6 multiply_reduce_fusion.5
  151.0 12.4 %copy.255 = f32[1,512,1536]{1,2,0:T(8,128)} copy(f32[1,512,1536]{2,1,0:T(8,128)} %mul.669) | data formatting | bytes 6291456 | tf_op jit(solution)/shard_map/transpose(jvp())/mul | solution.py:162
  163.4 5.4 fusion.107
  168.9 17.8 %all_gather.29 = f32[4,1,24]{2,1,0:T(1,128)} all-gather(f32[1,1,24]{2,1,0:T(1,128)S(1)} %copy-done.87), channel_id=1, replica_groups=mesh['dp'=8,'seq'=4] {'seq'}, dimensions={0}, use_global_device_ids=true | all-gather | bytes 480 | tf_op jit(solution)/shard_map/all_gather | solution.py:38
  186.7 3.5 copy.256
  190.2 3.7 multiply_reduce_fusion.6
  194.8 33.7 %fusion.7 = (f32[24,512]{1,0:T(8,128)}, f32[24,512]{1,0:T(8,128)S(1)}, f32[512,512]{1,0:T(8,128)}) fusion(f32[24,512]{1,0:T(8,128)} %bitcast_add_fusion.6, f32[512,512]{1,0:T(8,128)} %fusion.111, pred[512,512]{1,0:T(8,128)(4,1)} %fusion.81, f32[24,64,512]{2,1,0:T(8,128)} %bitcast.346, f32[512,24,64]{0,2,1:T(8,128)S(1)} %bitcast.339, f32[512,24]{0,1:T(8,128)} %copy.243), kind=kOutput, calls=%fused_computation.12 | convolution fusion | flops 4888961024 | bytes 8847360 | tf_op jit(solution)/shard_map/transpose(jvp(shtu,suhp->sthp))/dot_general | solution.py:157
  230.9 3.9 convolution_bitcast_fusion.1
  234.9 7.1 convolution_bitcast_fusion.2
  244.7 3.9 fusion.91
  248.6 22.4 %fusion.2 = f32[24,64,512]{2,1,0:T(8,128)} fusion(f32[24,64,512]{2,1,0:T(8,128)S(1)} %bitcast.347, f32[24,512]{1,0:T(8,128)S(1)} %copy-done.46, f32[512,512]{1,0:T(8,128)S(1)} %copy-done.28, pred[512,512]{1,0:T(8,128)(4,1)S(1)} %copy-done.33), kind=kOutput, calls=%fused_computation.9 | convolution fusion | flops 4850712576 | bytes 7651328 | tf_op jit(solution)/shard_map/transpose(jvp(shtu,suhp->sthp))/dot_general | solution.py:157
  271.0 12.0 %while.29 = (s32[]{:T(128)}, f32[1,24,64,128]{3,2,1,0:T(8,128)}, s32[]{:T(128)}, f32[4,1,24]{2,1,0:T(1,128)}, f32[4,1,24,64,128]{4,3,2,1,0:T(8,128)}, /*index=5*/s32[]{:T(128)}, s32[]{:T(128)}, s32[]{:T(128)}, s32[]{:T(128)}) while((s32[]{:T(128)}, f32[1,24,64,128]{3,2,1,0:T(8,128)}, s32[]{:T(128)}, f32[4,1,24]{2,1,0:T(1,128)}, ...), condition=%wide.region_11.12_spmd.clone, body=%wide.region_10.11_spmd.clone.sunk | while | flops 786440 | bytes 2359751 | solution.py:51
  283.0 4.1 fusion.34
  288.0 5.8 fusion.76
  293.8 4.2 fusion.33
  300.5 11.2 %multiply_reduce_fusion.3 = (f32[1792]{0:T(1024)}, f32[1792]{0:T(1024)S(1)}, f32[1792]{0:T(1024)}, f32[1792]{0:T(1024)S(1)}, f32[1792]{0:T(1024)}, /*index=5*/f32[1,512,1792]{2,1,0:T(8,128)S(1)}) fusion(f32[1,512,1792]{2,1,0:T(8,128)} %slice.132, f32[1,3,1792]{2,1,0:T(4,128)S(1)} %copy.241, f32[512]{0:T(512)S(1)} %bitcast.375, f32[512]{0:T(512)S(1)} %bitcast.369, ...), kind=kLoop, calls=%fused_computation.43 | loop fusion | flops 24763648 | bytes 18415616 | tf_op jit(solution)/shard_map/transpose(jvp())/reduce_sum | solution.py:119
  319.6 5.0 reduce-window.36
  324.8 5.0 reduce-window.34
  334.5 3.1 fusion.68
  337.7 5.8 pad_maximum_fusion
  343.4 15.2 %copy.289 = f32[768,4888]{1,0:T(8,128)} copy(f32[768,4888]{0,1:T(8,128)} %pad_maximum_fusion) | data formatting | bytes 30031872
  358.6 256.6 %reduce-scatter.4.cloned.1.call-done = f32[192,4888]{1,0:T(8,128)} async-done(((f32[768,4888]{1,0:T(8,128)}), f32[192,4888]{1,0:T(8,128)}) %reduce-scatter.4.cloned.1.call-update) | async-done | bytes 3754000
  615.2 5.7 copy.290
  622.9 89.6 %all-reduce.16.cloned.1.call-done = f32[192,4888]{0,1:T(8,128)} async-done(((f32[192,4888]{0,1:T(8,128)}), f32[192,4888]{0,1:T(8,128)}) %all-reduce.16.cloned.1.call-update) | async-done | bytes 3754000 | tf_op jit(solution)/shard_map/psum | solution.py:241
  712.5 3.5 subtract_convert_fusion.1
  717.1 3.6 copy.270
  720.7 6.4 subtract_convert_fusion
  727.1 3.8 copy.272
  731.3 3.3 multiply_reduce_fusion.8
  734.9 7.1 fusion.50
  742.6 42.8 %all-reduce.13 = (f32[768]{0:T(1024)}, f32[4,1792]{1,0:T(4,128)}, f32[1792]{0:T(1024)}, f32[24]{0:T(128)}, f32[24]{0:T(128)}, /*index=5*/f32[24]{0:T(128)}, f32[1536]{0:T(1024)}, f32[]{:T(128)}, f32[]{:T(128)}, f32[]{:T(128)}) all-reduce(f32[768]{0:T(1024)S(1)} %get-tuple-element.396, ...), channel_id=1, replica_groups=mesh['dp'=8,'seq'=4] {'dp','seq'}, use_global_device_ids=true, to_apply=%region_26.27 | all-reduce | flops 11339 | bytes 90712 | tf_op jit(solution)/shard_map/psum | solution.py:267
  787.5 3.3 fusion.52
  796.5 4.3 copy.276
  800.8 66.9 %all-gather.7.cloned.1.call-done = bf16[768,3352]{1,0:T(8,128)(2,1)} async-done(((bf16[192,3352]{1,0:T(8,128)(2,1)}), bf16[768,3352]{1,0:T(8,128)(2,1)}) %all-gather.7.cloned.1.call-update) | async-done | bytes 5148688 | tf_op jit(solution)/shard_map/all_gather | solution.py:253
  867.7 8.0 copy.275
  (306 shorter events, 82.4 us)
Async XLA Ops:
  7.2 88.0 %all-gather.11.cloned.1.call-start = ((), (), s32[]{:S(2)}) async-start(), calls=%async_computation.3 | async-start | bytes 1966080 | tf_op jit(solution)/shard_map/all_gather | solution.py:19
  9.2 5.6 copy-start.69
  9.2 10.6 %copy-start.72 = (s32[1,512]{1,0:T(1,128)S(1)}, s32[1,512]{1,0:T(1,128)}, u32[]{:S(2)}) copy-start(s32[1,512]{1,0:T(1,128)} %param.24) | copy-start | bytes 6148
  9.2 14.2 %copy-start.91 = (f32[24]{0:T(128)S(1)}, f32[24]{0:T(128)}, u32[]{:S(2)}) copy-start(f32[24]{0:T(128)} %param.34) | copy-start | bytes 292
  9.2 14.2 %copy-start.75 = (f32[24]{0:T(128)S(1)}, f32[24]{0:T(128)}, u32[]{:S(2)}) copy-start(f32[24]{0:T(128)} %param.33) | copy-start | bytes 292
  14.8 8.6 copy-start.4
  14.8 21.5 %collective-permute-start = (f32[1,3,1792]{2,0,1:T(1,128)S(1)}, f32[1,3,1792]{2,0,1:T(1,128)S(1)}, u32[]{:S(2)}, u32[]{:S(2)}) collective-permute-start(f32[1,3,1792]{2,0,1:T(1,128)S(1)} %copy.240), channel_id=1, source_target_pairs={{0,1},{1,2},{2,3},{4,5},{5,6},{6,7},{8,9},{9,10},{10,11},{12,13},{... | collective-permute-start | bytes 64520 | tf_op jit(solution)/shard_map/ppermute | solution.py:13
  19.9 16.3 %collective-permute-start.1 = (f32[1,3]{1,0:T(1,128)S(1)}, f32[1,3]{1,0:T(1,128)S(1)}, u32[]{:S(2)}, u32[]{:S(2)}) collective-permute-start(f32[1,3]{1,0:T(1,128)S(1)} %slice.135), channel_id=1, source_target_pairs={{0,1},{1,2},{2,3},{4,5},{5,6},{6,7},{8,9},{9,10},{10,11},{12,13},{... | collective-permute-start | bytes 44 | tf_op jit(solution)/shard_map/ppermute | solution.py:13
  25.8 10.2 %copy-start.63 = (f32[4,1792]{1,0:T(4,128)S(1)}, f32[4,1792]{1,0:T(4,128)}, u32[]{:S(2)}) copy-start(f32[4,1792]{1,0:T(4,128)} %param.31) | copy-start | bytes 86020
  25.8 10.5 %copy-start.74 = (f32[1792]{0:T(1024)S(1)}, f32[1792]{0:T(1024)}, u32[]{:S(2)}) copy-start(f32[1792]{0:T(1024)} %param.32) | copy-start | bytes 21508
  30.0 17.9 %copy-start.57 = (f32[1,512]{1,0:T(1,128)}, f32[1,512]{1,0:T(1,128)S(1)}, u32[]{:S(2)}) copy-start(f32[1,512]{1,0:T(1,128)S(1)} %compare_convert_fusion) | copy-start | bytes 6148
  30.8 17.1 %copy-start.62 = (s32[512]{0:T(512)}, s32[512]{0:T(512)S(1)}, u32[]{:S(2)}) copy-start(s32[512]{0:T(512)S(1)} %get-tuple-element.452) | copy-start | bytes 6148
  36.1 11.8 %copy-start.41 = (f32[1792]{0:T(1024)}, f32[1792]{0:T(1024)S(1)}, u32[]{:S(2)}) copy-start(f32[1792]{0:T(1024)S(1)} %get-tuple-element.401) | copy-start | bytes 21508
  36.2 11.8 %copy-start.43 = (f32[1792]{0:T(1024)}, f32[1792]{0:T(1024)S(1)}, u32[]{:S(2)}) copy-start(f32[1792]{0:T(1024)S(1)} %get-tuple-element.402) | copy-start | bytes 21508
  36.3 11.7 %copy-start.51 = (f32[1,512]{1,0:T(1,128)}, f32[1,512]{1,0:T(1,128)S(1)}, u32[]{:S(2)}) copy-start(f32[1,512]{1,0:T(1,128)S(1)} %get-tuple-element.470) | copy-start | bytes 6148
  36.3 11.7 %copy-start.53 = (f32[1,512]{1,0:T(1,128)}, f32[1,512]{1,0:T(1,128)S(1)}, u32[]{:S(2)}) copy-start(f32[1,512]{1,0:T(1,128)S(1)} %get-tuple-element.471) | copy-start | bytes 6148
  36.3 11.7 %copy-start.55 = (f32[1,512]{1,0:T(1,128)}, f32[1,512]{1,0:T(1,128)S(1)}, u32[]{:S(2)}) copy-start(f32[1,512]{1,0:T(1,128)S(1)} %get-tuple-element.472) | copy-start | bytes 6148
  58.7 212.3 %all-gather.13.cloned.1.call-start = ((), (), s32[]{:S(2)}) async-start(), calls=%async_computation.4 | async-start | bytes 3932160 | tf_op jit(solution)/shard_map/all_gather | solution.py:38
  100.4 29.4 %copy-start.14 = (f32[512,24,64]{0,2,1:T(8,128)}, f32[512,24,64]{0,2,1:T(8,128)S(1)}, u32[]{:S(2)}) copy-start(f32[512,24,64]{0,2,1:T(8,128)S(1)} %fusion.88) | copy-start | bytes 9437188
  141.5 7.3 copy-start.15
  163.4 5.5 copy-start.87
  168.8 446.4 %reduce-scatter.4.cloned.1.call-start = ((), (), s32[]{:S(2)}) async-start(), calls=%async_computation.6 | async-start | bytes 19169280
  230.9 11.1 %copy-start.18 = (f32[512,512]{1,0:T(8,128)S(1)}, f32[512,512]{1,0:T(8,128)}, u32[]{:S(2)}) copy-start(f32[512,512]{1,0:T(8,128)} %get-tuple-element.388) | copy-start | bytes 3145732
  230.9 13.7 %copy-start.7 = (f32[1,512,1536]{2,1,0:T(8,128)S(1)}, f32[1,512,1536]{2,1,0:T(8,128)}, u32[]{:S(2)}) copy-start(f32[1,512,1536]{2,1,0:T(8,128)} %copy-done.6) | copy-start | bytes 9437188
  230.9 13.7 %copy-start.17 = (bf16[1,512,768]{2,1,0:T(8,128)(2,1)S(1)}, bf16[1,512,768]{2,1,0:T(8,128)(2,1)}, u32[]{:S(2)}) copy-start(bf16[1,512,768]{2,1,0:T(8,128)(2,1)} %param.23) | copy-start | bytes 2359300
  230.9 13.7 %copy-start.48 = (f32[1536]{0:T(1024)S(1)}, f32[1536]{0:T(1024)}, u32[]{:S(2)}) copy-start(f32[1536]{0:T(1024)} %param.36) | copy-start | bytes 18436
  230.9 13.7 %copy-start.65 = (f32[512]{0:T(512)S(1)}, f32[512]{0:T(512)}, u32[]{:S(2)}) copy-start(f32[512]{0:T(512)} %copy-done.64) | copy-start | bytes 6148
  283.0 5.0 copy-start.29
  283.0 10.8 %copy-start.21 = (f32[24,64,512]{2,1,0:T(8,128)S(1)}, f32[24,64,512]{2,1,0:T(8,128)}, u32[]{:S(2)}) copy-start(f32[24,64,512]{2,1,0:T(8,128)} %fusion.2) | copy-start | bytes 9437188
  287.2 6.6 copy-start.11
  287.2 6.6 copy-start.37
  287.2 6.6 copy-start.90
  300.5 11.2 %copy-start.42 = (f32[1792]{0:T(1024)S(1)}, f32[1792]{0:T(1024)}, u32[]{:S(2)}) copy-start(f32[1792]{0:T(1024)} %copy-done.41) | copy-start | bytes 21508
  300.5 11.2 %copy-start.44 = (f32[1792]{0:T(1024)S(1)}, f32[1792]{0:T(1024)}, u32[]{:S(2)}) copy-start(f32[1792]{0:T(1024)} %copy-done.43) | copy-start | bytes 21508
  313.3 4.7 copy-start.30
  313.4 6.0 copy-start.86
  316.4 13.7 %copy-start.38 = (f32[512,24]{0,1:T(8,128)S(1)}, f32[512,24]{0,1:T(8,128)}, u32[]{:S(2)}) copy-start(f32[512,24]{0,1:T(8,128)} %get-tuple-element.466) | copy-start | bytes 147460
  316.4 13.9 %copy-start.85 = (f32[24]{0:T(128)S(1)}, f32[24]{0:T(128)}, u32[]{:S(2)}) copy-start(f32[24]{0:T(128)} %copy-done.84) | copy-start | bytes 292
  316.5 15.4 %collective-permute-start.2 = (bf16[1,3,1792]{2,1,0:T(4,128)(2,1)S(1)}, bf16[1,3,1792]{2,1,0:T(4,128)(2,1)S(1)}, u32[]{:S(2)}, u32[]{:S(2)}) collective-permute-start(bf16[1,3,1792]{2,1,0:T(4,128)(2,1)S(1)} %slice.284), channel_id=1, source_target_pairs={{1,0},{2,1},{3,2},{5,4},{6,5},{7,6},{9,8},{10,9},{11,10},{13,12},{... | collective-permute-start | bytes 32264 | tf_op jit(solution)/shard_map/ppermute | solution.py:13
  331.9 5.7 copy-start.39
  331.9 5.7 slice-start
  358.6 353.9 %all-reduce.16.cloned.1.call-start = ((), (), s32[]{:S(2)}) async-start(), calls=%async_computation.5 | async-start | bytes 10010624 | tf_op jit(solution)/shard_map/psum | solution.py:241
  621.0 175.6 %all-gather.9.cloned.1.call-start = ((), (), s32[]{:S(2)}) async-start(), calls=%async_computation.2 | async-start | bytes 2949120 | tf_op jit(solution)/shard_map/all_gather | solution.py:254
  717.1 150.7 %all-gather.7.cloned.1.call-start = ((), (), s32[]{:S(2)}) async-start(), calls=%async_computation.1 | async-start | bytes 6635520 | tf_op jit(solution)/shard_map/all_gather | solution.py:253
  734.8 7.2 copy-start.73
  734.8 7.8 copy-start.71
  734.9 52.6 %copy-start.68 = (f32[512]{0:T(512)S(1)}, f32[512]{0:T(512)}, u32[]{:S(2)}) copy-start(f32[512]{0:T(512)} %copy-done.67) | copy-start | bytes 6148
  742.0 48.8 %copy-start.13 = (f32[192,3352]{0,1:T(8,128)S(1)}, f32[192,3352]{0,1:T(8,128)}, u32[]{:S(2)}) copy-start(f32[192,3352]{0,1:T(8,128)} %get-tuple-element.444) | copy-start | bytes 7723012
  (56 other events, 191.2 us)
Sparse Core Ops, SparseCore 0:
  58.8 36.3 all-gather.10
  169.0 70.9 all-gather.12
  358.7 256.4 reduce-scatter.3
  621.1 91.3 all-reduce.15
  717.2 50.9 all-gather.8
  769.7 98.0 all-gather.6
where the time goes:
time: 895 us; the launch traced here: 885 us
  waiting for transfers between devices  421 us (47%)
  matrix products  151 us (17%)
  local copies, waits for them, and re-layouts  108 us (12%)
  other arithmetic  101 us (11%)
  blocking collectives  70.5 us (8%)
  between operations  23.1 us (3%)
  starting transfers between devices  10.1 us (1%)
    unnamed x7, waiting for transfers between devices  257 us
    psum x1, waiting for transfers between devices, local(): whole_grad = lax.psum(jnp.concatenate([in_part, out_part], axis=1), 'dp')  89.6 us
    dot_general x3, matrix products, piece_out(): jnp.einsum('shtu,suhp->sthp', weighted, signal_in * step_in[..., None], p...  85.3 us
    all_gather x1, waiting for transfers between devices, local(): lax.all_gather(new_in_part, 'seq', axis=0, tiled=True)  66.9 us
    unnamed x198, local copies, waits for them, and re-layouts  51 us
    psum x1, blocking collectives, local(): lax.psum((norm_gain_grad, conv_weight_grad, conv_bias_grad, dt_bias_grad,...  42.8 us
    mul x4, local copies, waits for them, and re-layouts, piece_out(): jnp.einsum('stn,shpn->sthp', reader_in, incoming_in, precision=highest)  20.4 us
  transfers between devices with their start and end apart: 9, of which 4 were waited for; matrix products, arithmetic and copies ran while one was open for 19% of the time, Pallas kernels for 0%

commit v1 on v0

--- a/solution.py
+++ b/solution.py
@@ -2,6 +2,7 @@
 import jax.numpy as jnp
 from jax import lax
 from jax.sharding import PartitionSpec as P
+from jax.lax import axis_index, axis_size, ppermute
 
 epsilon = 1e-05
 highest = lax.Precision.HIGHEST
@@ -83,6 +84,32 @@
     in_momentum,
     out_momentum,
 ):
+
+    def _create_yards(vector, comm_axis, on_dim):
+        local_next = axis_size(comm_axis)
+        n_now = axis_index(comm_axis)
+        wide_out, outer, state_next = (local_next, n_now, vector.shape[on_dim])
+        nodes = [(dev_j, (dev_j + 1) % wide_out) for dev_j in range(wide_out)]
+        near = jnp.zeros(
+            (*vector.shape[:on_dim], wide_out * state_next, *vector.shape[on_dim + 1 :]),
+            vector.dtype,
+        )
+        by_place = [(dev_j, (dev_j - 1) % wide_out) for dev_j in range(wide_out)]
+        z2 = item_now = vector
+        near = lax.dynamic_update_slice_in_dim(near, vector, outer * state_next, axis=on_dim)
+        a_now = wide_out // 2
+        for nth in range(1, a_now + 1):
+            z2 = ppermute(z2, comm_axis, perm=nodes)
+            near = lax.dynamic_update_slice_in_dim(
+                near, z2, (outer - nth) % wide_out * state_next, axis=on_dim
+            )
+            if nth < wide_out - a_now:
+                item_now = ppermute(item_now, comm_axis, by_place)
+                near = lax.dynamic_update_slice_in_dim(
+                    near, item_now, (outer + nth) % wide_out * state_next, axis=on_dim
+                )
+        return near
+
     seq_count, piece_size, model_width = tokens.shape
     head_count = dt_bias.shape[0]
     tap_count, channels = conv_weight.shape
@@ -250,7 +277,7 @@
     new_in_part = (own_in - rate_now * new_in_momentum).astype(jnp.bfloat16)
     new_out_part = (own_out - rate_now * new_out_momentum).astype(jnp.bfloat16)
     new_in_weight, new_out_weight = (
-        lax.all_gather(new_in_part, "seq", axis=0, tiled=True),
+        _create_yards(new_in_part, "seq", 0),
         lax.all_gather(new_out_part, "seq", axis=1, tiled=True),
     )
     (

time: 895 us -> 989 us (1.11)
  local copies, waits for them, and re-layouts: 108 us -> 182 us
  starting transfers between devices: 10.1 us -> 28.9 us
  blocking collectives: 70.5 us -> 87.3 us
  waiting for transfers between devices: 421 us -> 405 us
    dynamic_update_slice x0 -> x4, local copies, waits for them, and re-layouts: none -> 69.4 us  [the longest x2 34.1 us: _create_yards(): lax.dynamic_update_slice_in_dim(near, z2, (outer - nth) % wide_out * stat...]
    all_gather x1 -> x0, waiting for transfers between devices: 66.9 us -> none  [local(): lax.all_gather(new_in_part, 'seq', axis=0, tiled=True)]
    ppermute x0 -> x3, waiting for transfers between devices: none -> 54.8 us  [the longest x2 54.8 us: _create_yards(): z2 = ppermute(z2, comm_axis, perm=nodes)]
    ppermute x0 -> x3, starting transfers between devices: none -> 19 us  [the longest x2 16.7 us: _create_yards(): z2 = ppermute(z2, comm_axis, perm=nodes)]
    psum x1, blocking collectives: 42.8 us -> 60.3 us  [local(): lax.psum((norm_gain_grad, conv_weight_grad, conv_bias_grad, dt_bias_grad,...]
    unnamed x198 -> x209, local copies, waits for them, and re-layouts: 51 us -> 44.7 us
    unnamed x7 -> x6, waiting for transfers between devices: 257 us -> 257 us
  transfers between devices with their start and end apart: 9 -> 11, of which waited for: 4 -> 4; matrix products, arithmetic and copies ran while one was open for 19% -> 25% of each run, Pallas kernels for 0% -> 0%
where the time goes in v1:
time: 989 us; the launch traced here: 977 us
  waiting for transfers between devices  405 us (41%)
  local copies, waits for them, and re-layouts  182 us (18%)
  matrix products  151 us (15%)
  other arithmetic  100 us (10%)
  blocking collectives  87.3 us (9%)
  starting transfers between devices  28.9 us (3%)
  between operations  22.9 us (2%)
    unnamed x6, waiting for transfers between devices  257 us
    dot_general x3, matrix products, piece_out(): jnp.einsum('shtu,suhp->sthp', weighted, signal_in * step_in[..., None], p...  85.3 us
    psum x1, waiting for transfers between devices, local(): whole_grad = lax.psum(jnp.concatenate([in_part, out_part], axis=1), 'dp')  84.8 us
    psum x1, blocking collectives, local(): lax.psum((norm_gain_grad, conv_weight_grad, conv_bias_grad, dt_bias_grad,...  60.3 us
    ppermute x2, waiting for transfers between devices, _create_yards(): z2 = ppermute(z2, comm_axis, perm=nodes)  54.8 us
    unnamed x209, local copies, waits for them, and re-layouts  44.7 us
    dynamic_update_slice x2, local copies, waits for them, and re-layouts, _create_yards(): lax.dynamic_update_slice_in_dim(near, z2, (outer - nth) % wide_out * stat...  34.1 us
    mul x4, local copies, waits for them, and re-layouts, piece_out(): jnp.einsum('stn,shpn->sthp', reader_in, incoming_in, precision=highest)  20.4 us
  transfers between devices with their start and end apart: 11, of which 4 were waited for; matrix products, arithmetic and copies ran while one was open for 25% of the time, Pallas kernels for 0%

profile of v1, /device:TPU:0, one launch (start us, length us, event | category | flops | bytes accessed | tf_op | source)
XLA Modules:
  0.0 977.2 jit_solution(7025139243212119503)
XLA Ops:
  9.2 5.5 convolution_bitcast_fusion
  14.8 4.9 collective-permute-start
  25.9 4.2 slice.132
  36.4 11.4 %fusion.26 = (f32[1,512,1792]{2,1,0:T(8,128)S(1)}, f32[1,512,1792]{2,1,0:T(8,128)}) fusion(f32[1792]{0:T(1024)S(1)} %get-tuple-element.401, f32[1,512,1792]{2,1,0:T(8,128)} %slice.132, f32[512]{0:T(512)S(1)} %bitcast.377, f32[1792]{0:T(1024)S(1)} %get-tuple-element.402, f32[512]{0:T(512)S(1)} %bitcast.374, f32[1,3,1792]{2,1,0:T(4,128)S(1)} %copy.253, ...), kind=kLoop, calls=%fused_computation.50 | loop fusion | flops 17432576 | bytes 11075584 | tf_op jit(solution)/shard_map/jvp(jit(silu))/mul | solution.py:147
  54.1 4.3 fusion.70
  67.8 3.5 copy.266
  71.3 9.2 all_gather.23
  86.6 8.3 all-gather.8.cloned.1.call-done
  96.2 4.0 fusion.88
  100.3 29.3 %fusion.30 = f32[1,512,24,64]{1,3,2,0:T(8,128)} fusion(f32[1,512,24,64]{1,3,2,0:T(8,128)S(1)} %bitcast.337, f32[512,24,64]{0,2,1:T(8,128)S(1)} %fusion.88, f32[24]{0:T(128)S(1)} %copy-done.94, f32[512,24]{0,1:T(8,128)S(1)} %copy-done.38, f32[24,512]{1,0:T(8,128)S(1)} %copy-done.46, f32[512,512]{1,0:T(8,128)S(1)} %copy-done.30, ...), kind=kOutput, calls=%fused_computation.59 | convolution fusion | flops 4854644736 | bytes 14041184 | tf_op jit(solution)/shard_map/jvp(shtu,suhp->sthp)/dot_general | solution.py:184
  129.5 3.6 copy.264
  133.1 4.0 multiply_reduce_fusion.7
  141.2 5.6 multiply_reduce_fusion.5
  150.7 12.4 %copy.267 = f32[1,512,1536]{1,2,0:T(8,128)} copy(f32[1,512,1536]{2,1,0:T(8,128)} %mul.679) | data formatting | bytes 6291456 | tf_op jit(solution)/shard_map/transpose(jvp())/mul | solution.py:189
  163.1 5.4 fusion.107
  168.6 17.8 %all_gather.26 = f32[4,1,24]{2,1,0:T(1,128)} all-gather(f32[1,1,24]{2,1,0:T(1,128)S(1)} %copy-done.92), channel_id=1, replica_groups=mesh['dp'=8,'seq'=4] {'seq'}, dimensions={0}, use_global_device_ids=true | all-gather | bytes 480 | tf_op jit(solution)/shard_map/all_gather | solution.py:39
  186.4 3.5 copy.268
  189.9 3.7 multiply_reduce_fusion.6
  194.5 33.6 %fusion.7 = (f32[24,512]{1,0:T(8,128)}, f32[24,512]{1,0:T(8,128)S(1)}, f32[512,512]{1,0:T(8,128)}) fusion(f32[24,512]{1,0:T(8,128)} %bitcast_add_fusion.6, f32[512,512]{1,0:T(8,128)} %fusion.111, pred[512,512]{1,0:T(8,128)(4,1)} %fusion.81, f32[24,64,512]{2,1,0:T(8,128)} %bitcast.346, f32[512,24,64]{0,2,1:T(8,128)S(1)} %bitcast.339, f32[512,24]{0,1:T(8,128)} %copy.255), kind=kOutput, calls=%fused_computation.12 | convolution fusion | flops 4888961024 | bytes 8847360 | tf_op jit(solution)/shard_map/transpose(jvp(shtu,suhp->sthp))/dot_general | solution.py:184
  230.6 3.9 convolution_bitcast_fusion.1
  234.5 7.1 convolution_bitcast_fusion.2
  244.4 3.9 fusion.91
  248.3 22.4 %fusion.2 = f32[24,64,512]{2,1,0:T(8,128)} fusion(f32[24,64,512]{2,1,0:T(8,128)S(1)} %bitcast.347, f32[24,512]{1,0:T(8,128)S(1)} %copy-done.47, f32[512,512]{1,0:T(8,128)S(1)} %copy-done.31, pred[512,512]{1,0:T(8,128)(4,1)S(1)} %copy-done.36), kind=kOutput, calls=%fused_computation.9 | convolution fusion | flops 4850712576 | bytes 7651328 | tf_op jit(solution)/shard_map/transpose(jvp(shtu,suhp->sthp))/dot_general | solution.py:184
  270.7 12.0 %while.29 = (s32[]{:T(128)}, f32[1,24,64,128]{3,2,1,0:T(8,128)}, s32[]{:T(128)}, f32[4,1,24]{2,1,0:T(1,128)}, f32[4,1,24,64,128]{4,3,2,1,0:T(8,128)}, /*index=5*/s32[]{:T(128)}, s32[]{:T(128)}, s32[]{:T(128)}, s32[]{:T(128)}) while((s32[]{:T(128)}, f32[1,24,64,128]{3,2,1,0:T(8,128)}, s32[]{:T(128)}, f32[4,1,24]{2,1,0:T(1,128)}, ...), condition=%wide.region_11.12_spmd.clone, body=%wide.region_10.11_spmd.clone.sunk | while | flops 786440 | bytes 2359751 | solution.py:52
  282.7 4.1 fusion.34
  287.7 5.8 fusion.76
  293.5 4.2 fusion.33
  300.2 10.9 %multiply_reduce_fusion.3 = (f32[1792]{0:T(1024)}, f32[1792]{0:T(1024)}, f32[1792]{0:T(1024)}, f32[1792]{0:T(1024)}, f32[1792]{0:T(1024)}, /*index=5*/f32[1,512,1792]{2,1,0:T(8,128)S(1)}) fusion(f32[1,512,1792]{2,1,0:T(8,128)} %slice.132, f32[1,3,1792]{2,1,0:T(4,128)S(1)} %copy.253, f32[512]{0:T(512)S(1)} %bitcast.375, f32[512]{0:T(512)S(1)} %bitcast.369, ...), kind=kLoop, calls=%fused_computation.43 | loop fusion | flops 24763648 | bytes 18415616 | tf_op jit(solution)/shard_map/transpose(jvp())/reduce_sum | solution.py:146
  318.8 5.0 reduce-window.36
  324.0 5.0 reduce-window.34
  337.4 5.8 pad_maximum_fusion
  343.1 15.2 %copy.304 = f32[768,4888]{1,0:T(8,128)} copy(f32[768,4888]{0,1:T(8,128)} %pad_maximum_fusion) | data formatting | bytes 30031872
  358.4 256.6 %reduce-scatter.4.cloned.1.call-done = f32[192,4888]{1,0:T(8,128)} async-done(((f32[768,4888]{1,0:T(8,128)}), f32[192,4888]{1,0:T(8,128)}) %reduce-scatter.4.cloned.1.call-update) | async-done | bytes 3754000
  615.0 5.7 copy.305
  627.4 84.8 %all-reduce.16.cloned.1.call-done = f32[192,4888]{0,1:T(8,128)} async-done(((f32[192,4888]{0,1:T(8,128)}), f32[192,4888]{0,1:T(8,128)}) %all-reduce.16.cloned.1.call-update) | async-done | bytes 3754000 | tf_op jit(solution)/shard_map/psum | solution.py:268
  712.2 3.5 subtract_convert_fusion.1
  716.9 7.5 subtract_convert_fusion
  724.4 3.7 copy.284
  735.8 54.8 %collective-permute-done.3 = bf16[192,3352]{1,0:T(8,128)(2,1)} collective-permute-done((bf16[192,3352]{1,0:T(8,128)(2,1)}, bf16[192,3352]{1,0:T(8,128)(2,1)}, u32[]{:S(2)}, u32[]{:S(2)}) %collective-permute-start.3) | collective-permute-done | bytes 1287200 | tf_op jit(solution)/shard_map/ppermute | solution.py:102
  790.6 15.2 %collective-permute-start.5 = (bf16[192,3352]{1,0:T(8,128)(2,1)}, bf16[192,3352]{1,0:T(8,128)(2,1)}, u32[]{:S(2)}, u32[]{:S(2)}) collective-permute-start(bf16[192,3352]{1,0:T(8,128)(2,1)} %collective-permute-done.3), channel_id=1, source_target_pairs={{0,1},{1,2},{2,3},{3,0},{4,5},{5,6},{6,7},{7,4},{8,9},{9,10},{10,1... | collective-permute-start | bytes 3861512 | tf_op jit(solution)/shard_map/ppermute | solution.py:102
  805.9 6.7 fusion.50
  813.2 60.3 %all-reduce.13 = (f32[768]{0:T(1024)}, f32[4,1792]{1,0:T(4,128)}, f32[1792]{0:T(1024)}, f32[24]{0:T(128)}, f32[24]{0:T(128)}, /*index=5*/f32[24]{0:T(128)}, f32[1536]{0:T(1024)}, f32[]{:T(128)}, f32[]{:T(128)}, f32[]{:T(128)}) all-reduce(f32[768]{0:T(1024)S(1)} %get-tuple-element.396, ...), channel_id=1, replica_groups=mesh['dp'=8,'seq'=4] {'dp','seq'}, use_global_device_ids=true, to_apply=%region_26.27 | all-reduce | flops 11339 | bytes 90712 | tf_op jit(solution)/shard_map/psum | solution.py:294
  879.8 16.6 %dynamic_update_slice.12 = bf16[768,3352]{0,1:T(8,128)(2,1)} dynamic-update-slice(bf16[768,3352]{0,1:T(8,128)(2,1)} %broadcast_in_dim.133, bf16[192,3352]{0,1:T(8,128)(2,1)S(1)} %copy-done.12, s32[]{:T(128)S(6)} %select_n.153, s32[]{:T(128)} %constant.139.clone.1) | dynamic-update-slice | bytes 2574340 | tf_op jit(solution)/shard_map/dynamic_update_slice | solution.py:99
  896.3 4.9 copy.292
  905.4 17.9 %dynamic_update_slice.13 = bf16[768,3352]{0,1:T(8,128)(2,1)} dynamic-update-slice(bf16[768,3352]{0,1:T(8,128)(2,1)} %dynamic_update_slice.12, bf16[192,3352]{0,1:T(8,128)(2,1)S(1)} %copy.285, s32[]{:T(128)S(6)} %select_n.155, s32[]{:T(128)} %constant.139.clone.1) | dynamic-update-slice | bytes 2574340 | tf_op jit(solution)/shard_map/dynamic_update_slice | solution.py:103
  926.1 18.7 %dynamic_update_slice.14 = bf16[768,3352]{0,1:T(8,128)(2,1)} dynamic-update-slice(bf16[768,3352]{0,1:T(8,128)(2,1)} %dynamic_update_slice.13, bf16[192,3352]{0,1:T(8,128)(2,1)S(1)} %copy.287, s32[]{:T(128)S(6)} %select_n.157, s32[]{:T(128)} %constant.139.clone.1) | dynamic-update-slice | bytes 2574340 | tf_op jit(solution)/shard_map/dynamic_update_slice | solution.py:108
  947.5 16.2 %dynamic_update_slice.15 = bf16[768,3352]{0,1:T(8,128)(2,1)} dynamic-update-slice(bf16[768,3352]{0,1:T(8,128)(2,1)} %dynamic_update_slice.14, bf16[192,3352]{0,1:T(8,128)(2,1)S(1)} %copy.288, s32[]{:T(128)S(6)} %select_n.159, s32[]{:T(128)} %constant.139.clone.1) | dynamic-update-slice | bytes 2574340 | tf_op jit(solution)/shard_map/dynamic_update_slice | solution.py:103
  963.7 4.3 copy.291
  (328 shorter events, 109.1 us)
Async XLA Ops:
  7.2 87.7 %all-gather.8.cloned.1.call-start = ((), (), s32[]{:S(2)}) async-start(), calls=%async_computation.2 | async-start | bytes 1966080 | tf_op jit(solution)/shard_map/all_gather | solution.py:20
  9.2 10.6 %copy-start.76 = (s32[1,512]{1,0:T(1,128)S(1)}, s32[1,512]{1,0:T(1,128)}, u32[]{:S(2)}) copy-start(s32[1,512]{1,0:T(1,128)} %param.24) | copy-start | bytes 6148
  9.2 14.2 %copy-start.97 = (f32[24]{0:T(128)S(1)}, f32[24]{0:T(128)}, u32[]{:S(2)}) copy-start(f32[24]{0:T(128)} %param.34) | copy-start | bytes 292
  9.2 14.2 %copy-start.79 = (f32[24]{0:T(128)S(1)}, f32[24]{0:T(128)}, u32[]{:S(2)}) copy-start(f32[24]{0:T(128)} %param.33) | copy-start | bytes 292
  14.8 8.6 copy-start.4
  14.8 21.5 %collective-permute-start = (f32[1,3,1792]{2,0,1:T(1,128)S(1)}, f32[1,3,1792]{2,0,1:T(1,128)S(1)}, u32[]{:S(2)}, u32[]{:S(2)}) collective-permute-start(f32[1,3,1792]{2,0,1:T(1,128)S(1)} %copy.252), channel_id=1, source_target_pairs={{0,1},{1,2},{2,3},{4,5},{5,6},{6,7},{8,9},{9,10},{10,11},{12,13},{... | collective-permute-start | bytes 64520 | tf_op jit(solution)/shard_map/ppermute | solution.py:14
  19.9 16.3 %collective-permute-start.1 = (f32[1,3]{1,0:T(1,128)S(1)}, f32[1,3]{1,0:T(1,128)S(1)}, u32[]{:S(2)}, u32[]{:S(2)}) collective-permute-start(f32[1,3]{1,0:T(1,128)S(1)} %slice.135), channel_id=1, source_target_pairs={{0,1},{1,2},{2,3},{4,5},{5,6},{6,7},{8,9},{9,10},{10,11},{12,13},{... | collective-permute-start | bytes 44 | tf_op jit(solution)/shard_map/ppermute | solution.py:14
  25.8 10.2 %copy-start.66 = (f32[4,1792]{1,0:T(4,128)S(1)}, f32[4,1792]{1,0:T(4,128)}, u32[]{:S(2)}) copy-start(f32[4,1792]{1,0:T(4,128)} %param.31) | copy-start | bytes 86020
  25.8 10.5 %copy-start.78 = (f32[1792]{0:T(1024)S(1)}, f32[1792]{0:T(1024)}, u32[]{:S(2)}) copy-start(f32[1792]{0:T(1024)} %param.32) | copy-start | bytes 21508
  30.1 17.6 %copy-start.58 = (f32[1,512]{1,0:T(1,128)}, f32[1,512]{1,0:T(1,128)S(1)}, u32[]{:S(2)}) copy-start(f32[1,512]{1,0:T(1,128)S(1)} %compare_convert_fusion) | copy-start | bytes 6148
  30.9 16.8 %copy-start.65 = (s32[512]{0:T(512)}, s32[512]{0:T(512)S(1)}, u32[]{:S(2)}) copy-start(s32[512]{0:T(512)S(1)} %get-tuple-element.452) | copy-start | bytes 6148
  36.2 11.6 %copy-start.42 = (f32[1792]{0:T(1024)}, f32[1792]{0:T(1024)S(1)}, u32[]{:S(2)}) copy-start(f32[1792]{0:T(1024)S(1)} %get-tuple-element.401) | copy-start | bytes 21508
  36.2 11.6 %copy-start.44 = (f32[1792]{0:T(1024)}, f32[1792]{0:T(1024)S(1)}, u32[]{:S(2)}) copy-start(f32[1792]{0:T(1024)S(1)} %get-tuple-element.402) | copy-start | bytes 21508
  36.3 11.5 %copy-start.52 = (f32[1,512]{1,0:T(1,128)}, f32[1,512]{1,0:T(1,128)S(1)}, u32[]{:S(2)}) copy-start(f32[1,512]{1,0:T(1,128)S(1)} %get-tuple-element.470) | copy-start | bytes 6148
  36.3 11.5 %copy-start.54 = (f32[1,512]{1,0:T(1,128)}, f32[1,512]{1,0:T(1,128)S(1)}, u32[]{:S(2)}) copy-start(f32[1,512]{1,0:T(1,128)S(1)} %get-tuple-element.471) | copy-start | bytes 6148
  36.3 11.5 %copy-start.56 = (f32[1,512]{1,0:T(1,128)}, f32[1,512]{1,0:T(1,128)S(1)}, u32[]{:S(2)}) copy-start(f32[1,512]{1,0:T(1,128)S(1)} %get-tuple-element.472) | copy-start | bytes 6148
  58.4 212.3 %all-gather.10.cloned.1.call-start = ((), (), s32[]{:S(2)}) async-start(), calls=%async_computation.3 | async-start | bytes 3932160 | tf_op jit(solution)/shard_map/all_gather | solution.py:39
  100.2 29.4 %copy-start.14 = (f32[512,24,64]{0,2,1:T(8,128)}, f32[512,24,64]{0,2,1:T(8,128)S(1)}, u32[]{:S(2)}) copy-start(f32[512,24,64]{0,2,1:T(8,128)S(1)} %fusion.88) | copy-start | bytes 9437188
  168.6 446.4 %reduce-scatter.4.cloned.1.call-start = ((), (), s32[]{:S(2)}) async-start(), calls=%async_computation.5 | async-start | bytes 19169280
  230.6 11.1 %copy-start.20 = (f32[512,512]{1,0:T(8,128)S(1)}, f32[512,512]{1,0:T(8,128)}, u32[]{:S(2)}) copy-start(f32[512,512]{1,0:T(8,128)} %get-tuple-element.388) | copy-start | bytes 3145732
  230.6 13.7 %copy-start.7 = (f32[1,512,1536]{2,1,0:T(8,128)S(1)}, f32[1,512,1536]{2,1,0:T(8,128)}, u32[]{:S(2)}) copy-start(f32[1,512,1536]{2,1,0:T(8,128)} %copy-done.6) | copy-start | bytes 9437188
  230.6 13.7 %copy-start.18 = (bf16[1,512,768]{2,1,0:T(8,128)(2,1)S(1)}, bf16[1,512,768]{2,1,0:T(8,128)(2,1)}, u32[]{:S(2)}) copy-start(bf16[1,512,768]{2,1,0:T(8,128)(2,1)} %param.23) | copy-start | bytes 2359300
  230.6 13.7 %copy-start.49 = (f32[1536]{0:T(1024)S(1)}, f32[1536]{0:T(1024)}, u32[]{:S(2)}) copy-start(f32[1536]{0:T(1024)} %param.36) | copy-start | bytes 18436
  230.6 13.7 %copy-start.68 = (f32[512]{0:T(512)S(1)}, f32[512]{0:T(512)}, u32[]{:S(2)}) copy-start(f32[512]{0:T(512)} %copy-done.67) | copy-start | bytes 6148
  282.7 10.8 %copy-start.24 = (f32[24,64,512]{2,1,0:T(8,128)S(1)}, f32[24,64,512]{2,1,0:T(8,128)}, u32[]{:S(2)}) copy-start(f32[24,64,512]{2,1,0:T(8,128)} %fusion.2) | copy-start | bytes 9437188
  300.2 10.9 %copy-start.43 = (f32[1792]{0:T(1024)S(1)}, f32[1792]{0:T(1024)}, u32[]{:S(2)}) copy-start(f32[1792]{0:T(1024)} %copy-done.42) | copy-start | bytes 21508
  300.2 10.9 %copy-start.45 = (f32[1792]{0:T(1024)S(1)}, f32[1792]{0:T(1024)}, u32[]{:S(2)}) copy-start(f32[1792]{0:T(1024)} %copy-done.44) | copy-start | bytes 21508
  315.8 13.6 %copy-start.41 = (f32[512,24]{0,1:T(8,128)S(1)}, f32[512,24]{0,1:T(8,128)}, u32[]{:S(2)}) copy-start(f32[512,24]{0,1:T(8,128)} %get-tuple-element.466) | copy-start | bytes 147460
  315.8 15.8 %collective-permute-start.2 = (bf16[1,3,1792]{2,1,0:T(4,128)(2,1)S(1)}, bf16[1,3,1792]{2,1,0:T(4,128)(2,1)S(1)}, u32[]{:S(2)}, u32[]{:S(2)}) collective-permute-start(bf16[1,3,1792]{2,1,0:T(4,128)(2,1)S(1)} %slice.284), channel_id=1, source_target_pairs={{1,0},{2,1},{3,2},{5,4},{6,5},{7,6},{9,8},{10,9},{11,10},{13,12},{... | collective-permute-start | bytes 32264 | tf_op jit(solution)/shard_map/ppermute | solution.py:14
  358.4 353.9 %all-reduce.16.cloned.1.call-start = ((), (), s32[]{:S(2)}) async-start(), calls=%async_computation.4 | async-start | bytes 10010624 | tf_op jit(solution)/shard_map/psum | solution.py:268
  620.7 342.9 %all-gather.6.cloned.1.call-start = ((), (), s32[]{:S(2)}) async-start(), calls=%async_computation.1 | async-start | bytes 2949120 | tf_op jit(solution)/shard_map/all_gather | solution.py:281
  716.8 12.8 %copy-start.51 = (f32[1536]{0:T(1024)S(1)}, f32[1536]{0:T(1024)}, u32[]{:S(2)}) copy-start(f32[1536]{0:T(1024)} %get-tuple-element.436) | copy-start | bytes 18436
  716.8 13.0 %copy-start.8 = (f32[1,512,1536]{2,1,0:T(8,128)S(1)}, f32[1,512,1536]{2,1,0:T(8,128)}, u32[]{:S(2)}) copy-start(f32[1,512,1536]{2,1,0:T(8,128)} %copy-done.6) | copy-start | bytes 9437188
  716.8 13.0 %copy-start.50 = (f32[1536]{0:T(1024)S(1)}, f32[1536]{0:T(1024)}, u32[]{:S(2)}) copy-start(f32[1536]{0:T(1024)} %param.36) | copy-start | bytes 18436
  716.9 13.0 %copy-start.69 = (f32[512]{0:T(512)S(1)}, f32[512]{0:T(512)}, u32[]{:S(2)}) copy-start(f32[512]{0:T(512)} %copy-done.67) | copy-start | bytes 6148
  728.1 62.5 %collective-permute-start.3 = (bf16[192,3352]{1,0:T(8,128)(2,1)}, bf16[192,3352]{1,0:T(8,128)(2,1)}, u32[]{:S(2)}, u32[]{:S(2)}) collective-permute-start(bf16[192,3352]{1,0:T(8,128)(2,1)} %copy.284), channel_id=1, source_target_pairs={{0,1},{1,2},{2,3},{3,0},{4,5},{5,6},{6,7},{7,4},{8,9},{9,10},{10,1... | collective-permute-start | bytes 3861512 | tf_op jit(solution)/shard_map/ppermute | solution.py:102
  729.9 75.9 %copy-start.22 = (bf16[1,512,768]{2,1,0:T(8,128)(2,1)S(1)}, bf16[1,512,768]{2,1,0:T(8,128)(2,1)}, u32[]{:S(2)}) copy-start(bf16[1,512,768]{2,1,0:T(8,128)(2,1)} %param.22) | copy-start | bytes 2359300
  729.9 75.9 %copy-start.27 = (bf16[512,1792]{1,0:T(8,128)(2,1)S(1)}, bf16[512,1792]{1,0:T(8,128)(2,1)}, u32[]{:S(2)}) copy-start(bf16[512,1792]{1,0:T(8,128)(2,1)} %copy-done.26) | copy-start | bytes 5505028
  729.9 75.9 %copy-start.29 = (bf16[512,1536]{1,0:T(8,128)(2,1)S(1)}, bf16[512,1536]{1,0:T(8,128)(2,1)}, u32[]{:S(2)}) copy-start(bf16[512,1536]{1,0:T(8,128)(2,1)} %get-tuple-element.457) | copy-start | bytes 4718596
  730.0 75.8 %copy-start.74 = (f32[512]{0:T(512)S(1)}, f32[512]{0:T(512)}, u32[]{:S(2)}) copy-start(f32[512]{0:T(512)} %copy-done.72) | copy-start | bytes 6148
  730.0 75.8 %copy-start.88 = (f32[768]{0:T(1024)S(1)}, f32[768]{0:T(1024)}, u32[]{:S(2)}) copy-start(f32[768]{0:T(1024)} %param.29) | copy-start | bytes 9220
  733.5 189.8 %collective-permute-start.4 = (bf16[192,3352]{1,0:T(8,128)(2,1)}, bf16[192,3352]{1,0:T(8,128)(2,1)}, u32[]{:S(2)}, u32[]{:S(2)}) collective-permute-start(bf16[192,3352]{1,0:T(8,128)(2,1)} %copy.284), channel_id=1, source_target_pairs={{0,3},{1,0},{2,1},{3,2},{4,7},{5,4},{6,5},{7,6},{8,11},{9,8},{10,9... | collective-permute-start | bytes 3861512 | tf_op jit(solution)/shard_map/ppermute | solution.py:107
  790.6 154.2 %collective-permute-start.5 = (bf16[192,3352]{1,0:T(8,128)(2,1)}, bf16[192,3352]{1,0:T(8,128)(2,1)}, u32[]{:S(2)}, u32[]{:S(2)}) collective-permute-start(bf16[192,3352]{1,0:T(8,128)(2,1)} %collective-permute-done.3), channel_id=1, source_target_pairs={{0,1},{1,2},{2,3},{3,0},{4,5},{5,6},{6,7},{7,4},{8,9},{9,10},{10,1... | collective-permute-start | bytes 3861512 | tf_op jit(solution)/shard_map/ppermute | solution.py:102
  805.8 7.4 copy-start.60
  805.8 7.4 copy-start.75
  805.9 69.8 %copy-start.71 = (f32[512]{0:T(512)S(1)}, f32[512]{0:T(512)}, u32[]{:S(2)}) copy-start(f32[512]{0:T(512)} %copy-done.70) | copy-start | bytes 6148
  805.9 69.8 %copy-start.19 = (bf16[1,512,768]{2,1,0:T(8,128)(2,1)S(1)}, bf16[1,512,768]{2,1,0:T(8,128)(2,1)}, u32[]{:S(2)}) copy-start(bf16[1,512,768]{2,1,0:T(8,128)(2,1)} %param.23) | copy-start | bytes 2359300
  805.9 69.8 %copy-start.23 = (bf16[1,512,768]{2,1,0:T(8,128)(2,1)S(1)}, bf16[1,512,768]{2,1,0:T(8,128)(2,1)}, u32[]{:S(2)}) copy-start(bf16[1,512,768]{2,1,0:T(8,128)(2,1)} %param.22) | copy-start | bytes 2359300
  (64 other events, 250.9 us)
Sparse Core Ops, SparseCore 0:
  58.5 36.3 all-gather.7
  168.7 71.0 all-gather.9
  358.5 256.4 reduce-scatter.3
  620.8 91.3 all-reduce.15
  716.9 94.3 all-gather.5
